TPU v7x, 32 devices: a whole 2x2x4 slice. The times are simulated.
32 devices in a mesh: row: 8 (over z, y), col: 4 (over x, core).
Axes of the slice: x: 2, y: 2, z: 4, core: 2. Of those that a mesh axis runs over, the one named last changes fastest.
Arguments:
- left_act: bfloat16 [768, 128], P(('row', 'col')), may hold values from -540 to 540
- right_act: bfloat16 [768, 128], P(('row', 'col')), may hold values from -6 to 6
- norm_gain: float32 [128], replicated, may hold values from 0.25 to 1.75
- norm_bias: float32 [128], replicated, may hold values from -3 to 3
- w_in: bfloat16 [128, 512], replicated, may hold values from -0.5 to 0.5
- b_in: float32 [512], replicated, may hold values from -3 to 3
- w_out: bfloat16 [512, 128], replicated, may hold values from -0.25 to 0.25
- w_bins: bfloat16 [128, 64], replicated, may hold values from -0.5 to 0.5
- labels: int32 [768, 768], P('row', 'col'), may hold values from 0 to 63, as said below
Outputs:
- grad_left: float32 [768, 128], P(('row', 'col'))
- grad_right: float32 [768, 128], P('col')
- grad_w_in: float32 [128, 512], replicated
- grad_w_out: float32 [512, 128], replicated
- grad_w_bins: float32 [128, 64], replicated
Inputs may be any that keep to these rules, and one draw needn't show every extreme that they name: labels is symmetric: labels[i, j] equals labels[j, i].
All inputs are finite; a program needn't handle non-finite values.
Results may differ from a plain program's by a relative error of at most 0.00039.
Values may be sent and summed in bfloat16 or wider, within the bound.
A program may use at most 64 MiB of HBM per device.

v0:
```python
import jax
import jax.numpy as jnp
from jax import lax
from jax.sharding import PartitionSpec as P


def inner(first, second):
    return lax.dot_general(
        first, second, (((0,), (0,)), ((), ())), preferred_element_type=jnp.float32
    )


def outer(first, second):
    return lax.dot_general(
        first, second, (((1,), (1,)), ((), ())), preferred_element_type=jnp.float32
    )


def transition(left_rows, right_cols, gain, bias, w_in, b_in, w_out):
    summed = (
        left_rows.astype(jnp.float32)[:, None, :] + right_cols.astype(jnp.float32)[None, :, :]
    ).reshape(-1, left_rows.shape[1])
    center = summed - jnp.mean(summed, axis=-1, keepdims=True)
    inv_scale = lax.rsqrt(jnp.mean(center * center, axis=-1, keepdims=True) + 1e-05)
    normal_form = center * inv_scale
    normed = (normal_form * gain + bias).astype(jnp.bfloat16)
    pre_act = jnp.dot(normed, w_in, preferred_element_type=jnp.float32) + b_in
    hidden = (pre_act * jax.nn.sigmoid(pre_act)).astype(jnp.bfloat16)
    updated = (summed + jnp.dot(hidden, w_out, preferred_element_type=jnp.float32)).astype(
        jnp.bfloat16
    )
    return (normal_form, inv_scale, normed, pre_act, hidden, updated)


def pair_backward(sym, bin_labels, parts, gain, w_in, w_out, w_bins):
    normal_form, inv_scale, normed, pre_act, hidden, updated = parts
    shifted = sym - jnp.max(sym, axis=-1, keepdims=True)
    expo = jnp.exp(shifted)
    probs = expo / jnp.sum(expo, axis=-1, keepdims=True)
    onehot = (bin_labels[..., None] == lax.iota(jnp.int32, sym.shape[-1])).astype(jnp.float32)
    logit_grad = (2.0 * (probs - onehot)).reshape(-1, sym.shape[-1]).astype(jnp.bfloat16)
    grad_bins = inner(updated, logit_grad)
    upd_grad = outer(logit_grad, w_bins)
    upd_half = upd_grad.astype(jnp.bfloat16)
    grad_out = inner(hidden, upd_half)
    hid_grad = outer(upd_half, w_out)
    sigma = jax.nn.sigmoid(pre_act)
    pre_grad = (hid_grad * sigma * (1.0 + pre_act * (1.0 - sigma))).astype(jnp.bfloat16)
    grad_in = inner(normed, pre_grad)
    norm_grad = outer(pre_grad, w_in) * gain
    pair_grad = (
        inv_scale
        * (
            norm_grad
            - jnp.mean(norm_grad, axis=-1, keepdims=True)
            - normal_form * jnp.mean(norm_grad * normal_form, axis=-1, keepdims=True)
        )
        + upd_grad
    )
    return (grad_in, grad_out, grad_bins, pair_grad)


def on_device(left_act, right_act, norm_gain, norm_bias, w_in, b_in, w_out, w_bins, labels):
    tile_rows, tile_cols = labels.shape
    width = left_act.shape[1]
    stacked = jnp.stack([left_act, right_act])
    everything = lax.all_gather(stacked, ("row", "col"), axis=1, tiled=True)
    row_block = lax.dynamic_slice_in_dim(
        everything, lax.axis_index("row") * tile_rows, tile_rows, 1
    )
    column_block = lax.dynamic_slice_in_dim(
        everything, lax.axis_index("col") * tile_cols, tile_cols, 1
    )
    stride_rows = 8
    groups = tile_rows // stride_rows

    def advance(running, record):
        left_rows, right_rows, bin_labels = record
        own_parts = transition(left_rows, column_block[1], norm_gain, norm_bias, w_in, b_in, w_out)
        own_logits = jnp.dot(own_parts[5], w_bins, preferred_element_type=jnp.float32).reshape(
            stride_rows, tile_cols, -1
        )
        far_parts = transition(column_block[0], right_rows, norm_gain, norm_bias, w_in, b_in, w_out)
        far_logits = jnp.dot(far_parts[5], w_bins, preferred_element_type=jnp.float32).reshape(
            tile_cols, stride_rows, -1
        )
        sym = own_logits + jnp.transpose(far_logits, (1, 0, 2))
        grads = pair_backward(sym, bin_labels, own_parts, norm_gain, w_in, w_out, w_bins)
        pair_grad = grads[3].reshape(stride_rows, tile_cols, width)
        running = (
            running[0] + grads[0],
            running[1] + grads[1],
            running[2] + grads[2],
            running[3] + jnp.sum(pair_grad, axis=0),
        )
        return (running, jnp.sum(pair_grad, axis=1))

    start = (
        jnp.zeros((width, w_in.shape[1]), jnp.float32),
        jnp.zeros((w_in.shape[1], width), jnp.float32),
        jnp.zeros((width, w_bins.shape[1]), jnp.float32),
        jnp.zeros((tile_cols, width), jnp.float32),
    )
    records = (
        row_block[0].reshape(groups, stride_rows, width),
        row_block[1].reshape(groups, stride_rows, width),
        labels.reshape(groups, stride_rows, tile_cols),
    )
    running, left_terms = lax.scan(advance, start, records)
    grad_left = lax.psum_scatter(
        left_terms.reshape(tile_rows, width), "col", scatter_dimension=0, tiled=True
    )
    grad_right = lax.psum(running[3], "row")
    grad_in, grad_out, grad_bins = lax.psum((running[0], running[1], running[2]), ("row", "col"))
    residues = tile_rows * lax.axis_size("row")
    return (grad_left, grad_right, grad_in / residues, grad_out / residues, grad_bins / residues)


def solution(mesh):
    placed = (
        P(("row", "col"), None),
        P(("row", "col"), None),
        P(),
        P(),
        P(),
        P(),
        P(),
        P(),
        P("row", "col"),
    )
    return jax.shard_map(
        on_device,
        mesh=mesh,
        in_specs=placed,
        out_specs=(P(("row", "col"), None), P("col", None), P(), P(), P()),
        check_vma=False,
    )
```

profile of v0, /device:TPU:0, one launch (start us, length us, event | category | flops | bytes accessed | tf_op | source)
XLA Modules:
  0.0 632.4 jit_solution(9450483110087516917)
XLA Ops:
  8.8 44.3 %all_gather.3 = bf16[2,768,128]{2,1,0:T(8,128)(2,1)S(1)} all-gather(bf16[2,24,128]{2,1,0:T(8,128)(2,1)S(1)} %pad_maximum_fusion), channel_id=1, replica_groups=mesh['row'=8,'col'=4] {'row','col'}, dimensions={1}, use_global_device_ids=true | all-gather | bytes 405504 | tf_op jit(solution)/shard_map/all_gather | solution.py:67
  54.4 369.4 %while.19 = (s32[]{:T(128)}, f32[128,512]{1,0:T(8,128)}, f32[512,128]{1,0:T(8,128)S(1)}, f32[128,64]{0,1:T(8,128)}, f32[192,128]{1,0:T(8,128)}, /*index=5*/f32[1...) while((s32[]{:T(128)}, f32[128,512]{1,0:T(8,128)}, ...), condition=%wide.region_11.12_spmd.clone, body=%wide.region_0.11_spmd.clone.sunk | while | flops 1737784448 | bytes 44289180 | solution.py:109
  58.9 3.2 fusion.120
  63.3 2.6 multiply_convert_fusion.3
  69.9 5.1 fusion.121
  74.9 1.4 copy.32
  77.1 3.5 fusion.123
  89.7 3.2 fusion.120
  94.1 2.6 multiply_convert_fusion.3
  100.7 5.1 fusion.121
  107.9 3.5 fusion.123
  120.5 3.2 fusion.120
  124.9 2.6 multiply_convert_fusion.3
  131.5 5.1 fusion.121
  136.5 1.4 copy.32
  138.7 3.5 fusion.123
  151.3 3.2 fusion.120
  155.7 2.6 multiply_convert_fusion.3
  162.3 5.1 fusion.121
  169.5 3.5 fusion.123
  182.1 3.2 fusion.120
  186.5 2.6 multiply_convert_fusion.3
  193.0 5.1 fusion.121
  198.1 1.4 copy.32
  200.3 3.5 fusion.123
  212.8 3.2 fusion.120
  217.3 2.6 multiply_convert_fusion.3
  223.8 5.1 fusion.121
  228.9 1.4 copy.32
  231.1 3.5 fusion.123
  243.6 3.2 fusion.120
  248.1 2.6 multiply_convert_fusion.3
  254.6 5.1 fusion.121
  259.7 1.4 copy.32
  261.9 3.5 fusion.123
  274.4 3.2 fusion.120
  278.9 2.6 multiply_convert_fusion.3
  285.4 5.1 fusion.121
  290.4 1.4 copy.32
  292.6 3.5 fusion.123
  305.2 3.2 fusion.120
  309.6 2.6 multiply_convert_fusion.3
  316.2 5.1 fusion.121
  323.4 3.5 fusion.123
  336.0 3.2 fusion.120
  340.4 2.6 multiply_convert_fusion.3
  346.9 5.1 fusion.121
  352.0 1.4 copy.32
  354.2 3.5 fusion.123
  366.7 3.2 fusion.120
  371.2 2.6 multiply_convert_fusion.3
  377.7 5.1 fusion.121
  382.8 1.4 copy.32
  385.0 3.5 fusion.123
  397.5 3.2 fusion.120
  402.0 2.6 multiply_convert_fusion.3
  408.5 5.1 fusion.121
  415.8 3.5 fusion.123
  425.9 37.2 %psum.31 = f32[128,64]{0,1:T(8,128)S(1)} all-reduce(f32[128,64]{0,1:T(8,128)} %get-tuple-element.95), channel_id=1, replica_groups=mesh['row'=8,'col'=4] {'row','col'}, use_global_device_ids=true, to_apply=%region_16.17 | all-reduce | flops 8192 | bytes 65536 | tf_op jit(solution)/shard_map/psum | solution.py:114
  463.7 86.6 %all-reduce.7.cloned.1.call-done = (f32[128,512]{1,0:T(8,128)}, f32[512,128]{1,0:T(8,128)}) async-done(((f32[128,512]{1,0:T(8,128)}, f32[512,128]{1,0:T(8,128)}), (f32[128,512]{1,0:T(8,128)}, f32[512,128]{1,0:T(8,128)})) %all-reduce.7.cloned.1.call-update) | async-done | bytes 524304 | tf_op jit(solution)/shard_map/psum | solution.py:114
  550.3 1.7 broadcast_multiply_fusion.5
  552.0 1.7 broadcast_multiply_fusion.4
  553.7 69.8 %all-reduce.5.cloned.1.call-done = f32[192,128]{1,0:T(8,128)} async-done(((f32[192,128]{1,0:T(8,128)}), f32[192,128]{1,0:T(8,128)}) %all-reduce.5.cloned.1.call-update) | async-done | bytes 98320 | tf_op jit(solution)/shard_map/psum | solution.py:113
  623.4 1.5 copy.55
  (826 shorter events, 186.1 us)
Async XLA Ops:
  8.0 542.3 %all-reduce.7.cloned.1.call-start = ((), (), s32[]{:S(2)}) async-start(), calls=%async_computation.3 | async-start | bytes 1048576 | tf_op jit(solution)/shard_map/psum | solution.py:114
  58.9 4.4 copy-start.7
  58.9 4.4 copy-start.17
  69.9 6.7 %copy-start.12 = (f32[128,64]{0,1:T(8,128)S(1)}, f32[128,64]{0,1:T(8,128)}, u32[]{:S(2)}) copy-start(f32[128,64]{0,1:T(8,128)} %get-tuple-element.372) | copy-start | bytes 98308 | tf_op jit(solution)/shard_map/while
  69.9 6.9 %copy-start.11 = (bf16[128,64]{0,1:T(8,128)(2,1)S(1)}, bf16[128,64]{0,1:T(8,128)(2,1)}, u32[]{:S(2)}) copy-start(bf16[128,64]{0,1:T(8,128)(2,1)} %get-tuple-element.400) | copy-start | bytes 49156 | tf_op jit(solution)/shard_map/while
  77.1 4.2 copy-start.3
  89.6 4.4 copy-start.7
  89.7 4.4 copy-start.17
  100.6 6.7 %copy-start.12 = (f32[128,64]{0,1:T(8,128)S(1)}, f32[128,64]{0,1:T(8,128)}, u32[]{:S(2)}) copy-start(f32[128,64]{0,1:T(8,128)} %get-tuple-element.372) | copy-start | bytes 98308 | tf_op jit(solution)/shard_map/while
  100.7 6.9 %copy-start.11 = (bf16[128,64]{0,1:T(8,128)(2,1)S(1)}, bf16[128,64]{0,1:T(8,128)(2,1)}, u32[]{:S(2)}) copy-start(bf16[128,64]{0,1:T(8,128)(2,1)} %get-tuple-element.400) | copy-start | bytes 49156 | tf_op jit(solution)/shard_map/while
  107.9 4.2 copy-start.3
  120.4 4.4 copy-start.7
  120.4 4.4 copy-start.17
  131.5 6.7 %copy-start.12 = (f32[128,64]{0,1:T(8,128)S(1)}, f32[128,64]{0,1:T(8,128)}, u32[]{:S(2)}) copy-start(f32[128,64]{0,1:T(8,128)} %get-tuple-element.372) | copy-start | bytes 98308 | tf_op jit(solution)/shard_map/while
  131.5 6.9 %copy-start.11 = (bf16[128,64]{0,1:T(8,128)(2,1)S(1)}, bf16[128,64]{0,1:T(8,128)(2,1)}, u32[]{:S(2)}) copy-start(bf16[128,64]{0,1:T(8,128)(2,1)} %get-tuple-element.400) | copy-start | bytes 49156 | tf_op jit(solution)/shard_map/while
  138.7 4.2 copy-start.3
  151.2 4.0 copy-start.14
  151.2 4.4 copy-start.7
  151.3 4.4 copy-start.17
  162.3 6.7 %copy-start.12 = (f32[128,64]{0,1:T(8,128)S(1)}, f32[128,64]{0,1:T(8,128)}, u32[]{:S(2)}) copy-start(f32[128,64]{0,1:T(8,128)} %get-tuple-element.372) | copy-start | bytes 98308 | tf_op jit(solution)/shard_map/while
  162.3 6.9 %copy-start.11 = (bf16[128,64]{0,1:T(8,128)(2,1)S(1)}, bf16[128,64]{0,1:T(8,128)(2,1)}, u32[]{:S(2)}) copy-start(bf16[128,64]{0,1:T(8,128)(2,1)} %get-tuple-element.400) | copy-start | bytes 49156 | tf_op jit(solution)/shard_map/while
  169.5 4.2 copy-start.3
  182.0 4.4 copy-start.7
  182.1 4.4 copy-start.17
  193.0 6.7 %copy-start.12 = (f32[128,64]{0,1:T(8,128)S(1)}, f32[128,64]{0,1:T(8,128)}, u32[]{:S(2)}) copy-start(f32[128,64]{0,1:T(8,128)} %get-tuple-element.372) | copy-start | bytes 98308 | tf_op jit(solution)/shard_map/while
  193.0 6.9 %copy-start.11 = (bf16[128,64]{0,1:T(8,128)(2,1)S(1)}, bf16[128,64]{0,1:T(8,128)(2,1)}, u32[]{:S(2)}) copy-start(bf16[128,64]{0,1:T(8,128)(2,1)} %get-tuple-element.400) | copy-start | bytes 49156 | tf_op jit(solution)/shard_map/while
  200.3 4.2 copy-start.3
  212.8 4.4 copy-start.7
  212.8 4.4 copy-start.17
  223.8 6.7 %copy-start.12 = (f32[128,64]{0,1:T(8,128)S(1)}, f32[128,64]{0,1:T(8,128)}, u32[]{:S(2)}) copy-start(f32[128,64]{0,1:T(8,128)} %get-tuple-element.372) | copy-start | bytes 98308 | tf_op jit(solution)/shard_map/while
  223.8 6.9 %copy-start.11 = (bf16[128,64]{0,1:T(8,128)(2,1)S(1)}, bf16[128,64]{0,1:T(8,128)(2,1)}, u32[]{:S(2)}) copy-start(bf16[128,64]{0,1:T(8,128)(2,1)} %get-tuple-element.400) | copy-start | bytes 49156 | tf_op jit(solution)/shard_map/while
  231.1 4.2 copy-start.3
  243.6 4.4 copy-start.7
  243.6 4.4 copy-start.17
  254.6 6.7 %copy-start.12 = (f32[128,64]{0,1:T(8,128)S(1)}, f32[128,64]{0,1:T(8,128)}, u32[]{:S(2)}) copy-start(f32[128,64]{0,1:T(8,128)} %get-tuple-element.372) | copy-start | bytes 98308 | tf_op jit(solution)/shard_map/while
  254.6 6.9 %copy-start.11 = (bf16[128,64]{0,1:T(8,128)(2,1)S(1)}, bf16[128,64]{0,1:T(8,128)(2,1)}, u32[]{:S(2)}) copy-start(bf16[128,64]{0,1:T(8,128)(2,1)} %get-tuple-element.400) | copy-start | bytes 49156 | tf_op jit(solution)/shard_map/while
  261.9 4.2 copy-start.3
  274.4 4.4 copy-start.7
  274.4 4.4 copy-start.17
  285.4 6.7 %copy-start.12 = (f32[128,64]{0,1:T(8,128)S(1)}, f32[128,64]{0,1:T(8,128)}, u32[]{:S(2)}) copy-start(f32[128,64]{0,1:T(8,128)} %get-tuple-element.372) | copy-start | bytes 98308 | tf_op jit(solution)/shard_map/while
  285.4 6.9 %copy-start.11 = (bf16[128,64]{0,1:T(8,128)(2,1)S(1)}, bf16[128,64]{0,1:T(8,128)(2,1)}, u32[]{:S(2)}) copy-start(bf16[128,64]{0,1:T(8,128)(2,1)} %get-tuple-element.400) | copy-start | bytes 49156 | tf_op jit(solution)/shard_map/while
  292.6 4.2 copy-start.3
  305.2 4.4 copy-start.7
  305.2 4.4 copy-start.17
  316.2 6.7 %copy-start.12 = (f32[128,64]{0,1:T(8,128)S(1)}, f32[128,64]{0,1:T(8,128)}, u32[]{:S(2)}) copy-start(f32[128,64]{0,1:T(8,128)} %get-tuple-element.372) | copy-start | bytes 98308 | tf_op jit(solution)/shard_map/while
  316.2 6.9 %copy-start.11 = (bf16[128,64]{0,1:T(8,128)(2,1)S(1)}, bf16[128,64]{0,1:T(8,128)(2,1)}, u32[]{:S(2)}) copy-start(bf16[128,64]{0,1:T(8,128)(2,1)} %get-tuple-element.400) | copy-start | bytes 49156 | tf_op jit(solution)/shard_map/while
  323.4 4.2 copy-start.3
  335.9 4.4 copy-start.7
  336.0 4.4 copy-start.17
  346.9 6.7 %copy-start.12 = (f32[128,64]{0,1:T(8,128)S(1)}, f32[128,64]{0,1:T(8,128)}, u32[]{:S(2)}) copy-start(f32[128,64]{0,1:T(8,128)} %get-tuple-element.372) | copy-start | bytes 98308 | tf_op jit(solution)/shard_map/while
  346.9 6.9 %copy-start.11 = (bf16[128,64]{0,1:T(8,128)(2,1)S(1)}, bf16[128,64]{0,1:T(8,128)(2,1)}, u32[]{:S(2)}) copy-start(bf16[128,64]{0,1:T(8,128)(2,1)} %get-tuple-element.400) | copy-start | bytes 49156 | tf_op jit(solution)/shard_map/while
  354.2 4.2 copy-start.3
  366.7 4.4 copy-start.7
  366.7 4.4 copy-start.17
  377.7 6.7 %copy-start.12 = (f32[128,64]{0,1:T(8,128)S(1)}, f32[128,64]{0,1:T(8,128)}, u32[]{:S(2)}) copy-start(f32[128,64]{0,1:T(8,128)} %get-tuple-element.372) | copy-start | bytes 98308 | tf_op jit(solution)/shard_map/while
  377.7 6.9 %copy-start.11 = (bf16[128,64]{0,1:T(8,128)(2,1)S(1)}, bf16[128,64]{0,1:T(8,128)(2,1)}, u32[]{:S(2)}) copy-start(bf16[128,64]{0,1:T(8,128)(2,1)} %get-tuple-element.400) | copy-start | bytes 49156 | tf_op jit(solution)/shard_map/while
  385.0 4.2 copy-start.3
  397.5 4.4 copy-start.7
  397.5 4.4 copy-start.17
  408.5 6.7 %copy-start.12 = (f32[128,64]{0,1:T(8,128)S(1)}, f32[128,64]{0,1:T(8,128)}, u32[]{:S(2)}) copy-start(f32[128,64]{0,1:T(8,128)} %get-tuple-element.372) | copy-start | bytes 98308 | tf_op jit(solution)/shard_map/while
  408.5 6.9 %copy-start.11 = (bf16[128,64]{0,1:T(8,128)(2,1)S(1)}, bf16[128,64]{0,1:T(8,128)(2,1)}, u32[]{:S(2)}) copy-start(bf16[128,64]{0,1:T(8,128)(2,1)} %get-tuple-element.400) | copy-start | bytes 49156 | tf_op jit(solution)/shard_map/while
  415.8 4.2 copy-start.3
  424.5 129.1 %reduce-scatter.4.cloned.1.call-start = ((), (), s32[]{:S(2)}) async-start(), calls=%async_computation.2 | async-start | bytes 61440
  425.1 198.3 %all-reduce.5.cloned.1.call-start = ((), (), s32[]{:S(2)}) async-start(), calls=%async_computation.1 | async-start | bytes 196608 | tf_op jit(solution)/shard_map/psum | solution.py:113
  (144 other events, 347.9 us)
Sparse Core Ops, SparseCore 0:
  424.7 125.5 all-reduce.6
  554.2 69.1 all-reduce.4
Sparse Core Ops, SparseCore 1:
  428.0 15.6 reduce-scatter.3
where the time goes:
time: 636 us; the launch traced here: 632 us
  matrix products  222 us (35%)
  waiting for transfers between devices  158 us (25%)
  local copies, waits for them, and re-layouts  85.1 us (13%)
  blocking collectives  81.5 us (13%)
  other arithmetic  65.9 us (10%)
  between operations  15.5 us (2%)
    psum x1, waiting for transfers between devices, on_device(): lax.psum((running[0], running[1], running[2]), ('row', 'col'))  86.6 us
    psum x1, waiting for transfers between devices, on_device(): grad_right = lax.psum(running[3], 'row')  69.8 us
    div x12, matrix products, pair_backward(): probs = expo / jnp.sum(expo, axis=-1, keepdims=True)  60.6 us
    dot_general x36, matrix products, outer(): lax.dot_general(first, second, (((1,), (1,)), ((), ())), preferred_elemen...  57.6 us
    dot_general x24, matrix products, transition(): jnp.dot(hidden, w_out, preferred_element_type=jnp.float32)  45.4 us
    all_gather x1, blocking collectives, on_device(): everything = lax.all_gather(stacked, ('row', 'col'), axis=1, tiled=True)  44.3 us
    psum x1, blocking collectives, on_device(): lax.psum((running[0], running[1], running[2]), ('row', 'col'))  37.2 us
    dot_general x12, matrix products, transition(): pre_act = jnp.dot(normed, w_in, preferred_element_type=jnp.float32) + b_in  30.8 us
  transfers between devices with their start and end apart: 3, of which 2 were waited for; matrix products, arithmetic and copies ran while one was open for 1% of the time, Pallas kernels for 0%

commit v1 on v0

v1 whole, which is shorter than its diff:
```python
import jax
import jax.numpy as jnp
import numpy as np
from jax import lax
from jax.experimental import pallas as pl
from jax.experimental.pallas import tpu as pltpu
from jax.sharding import PartitionSpec as P

UNITS = 6
SUB = 8
F32 = jnp.float32
BF16 = jnp.bfloat16


def dims(first, second):
    return (((first,), (second,)), ((), ()))


def schedule(rows, cols, tile_rows, tile_cols):
    plans = []
    for r in range(rows):
        for c in range(cols):
            plan = []
            for i in range(tile_rows // SUB):
                for j in range(tile_cols // SUB):
                    big_i = r * tile_rows // SUB + i
                    big_j = c * tile_cols // SUB + j
                    if big_i == big_j:
                        plan.append((i, j, 1))
                    elif ((big_i + big_j) % 2 == 1) == (big_j > big_i):
                        plan.append((i, j, 2))
            plans.append(plan)
    longest = -(-max(map(len, plans)) // UNITS) * UNITS
    table = np.zeros((len(plans), 3, longest + 1), np.int32)
    for place, plan in enumerate(plans):
        table[place, :, : len(plan)] = np.array(plan, np.int32).T
        table[place, 0, longest] = -(-len(plan) // UNITS)
    return table


def pair_kernel(
    tab, left_i, right_i, left_j, right_j, gain_ref, bias_ref, w_in_h, b_h, w_out_ref, w_in_t,
    w_out_t_h, bins_t2, bins_t, lab,
    g_in, g_out, g_bins, o_left_i, o_right_i, o_left_j, o_right_j,
    raw_li, raw_ri, cen_li, cen_ri, raw_lj, raw_rj, cen_lj, cen_rj, acc_li, acc_ri, acc_bins,
):
    width = gain_ref.shape[1]
    scale = 1.0 / width
    half = UNITS * SUB * SUB
    last = tab.shape[1] - 1
    col_blocks = left_j.shape[0] // SUB

    for source, raw, cen in ((left_i, raw_li, cen_li), (right_i, raw_ri, cen_ri)):
        value = source[...].astype(F32)
        mid = value - jnp.sum(value, axis=-1, keepdims=True) * scale
        raw[...] = jnp.broadcast_to(value[:, None, :], raw.shape)
        cen[...] = jnp.broadcast_to(mid[:, None, :], cen.shape)
    for source, raw, cen in ((left_j, raw_lj, cen_lj), (right_j, raw_rj, cen_rj)):
        value = source[...].astype(F32)
        raw[...] = value
        cen[...] = value - jnp.sum(value, axis=-1, keepdims=True) * scale
    for ref in (g_in, g_out, acc_bins, o_left_j, o_right_j, acc_li, acc_ri):
        ref[...] = jnp.zeros_like(ref)

    lane = lax.broadcasted_iota(jnp.int32, (1, 2 * SUB * SUB), 1)
    first_half = lane < SUB * SUB

    def step(s, carry):
        places = [(tab[0, s * UNITS + u], tab[1, s * UNITS + u]) for u in range(UNITS)]
        rows = [pl.ds(pl.multiple_of(i * SUB, SUB), SUB) for i, j in places]
        cols = [pl.ds(pl.multiple_of(j * SUB, SUB), SUB) for i, j in places]

        def grid(li, rj, ri, lj):
            own = [(li[a] + rj[b][None]).reshape(SUB * SUB, width) for a, b in zip(rows, cols)]
            far = [(ri[a] + lj[b][None]).reshape(SUB * SUB, width) for a, b in zip(rows, cols)]
            return jnp.concatenate(own + far, axis=0)

        center = grid(cen_li, cen_rj, cen_ri, cen_lj)
        inv = lax.rsqrt(jnp.sum(center * center, axis=-1, keepdims=True) * scale + 1e-05)
        form = center * inv
        normed = (form * gain_ref[...] + bias_ref[...]).astype(BF16)
        u = jnp.dot(normed, w_in_h[...], preferred_element_type=F32) + b_h[...]
        t = jnp.tanh(u)
        up = 1.0 + t
        act = u * up
        slope = up + act * (1.0 - t)
        hidden = act.astype(BF16)
        updated = (
            grid(raw_li, raw_rj, raw_ri, raw_lj)
            + jnp.dot(hidden, w_out_ref[...], preferred_element_type=F32)
        ).astype(BF16)
        both = jnp.concatenate([updated[:half], updated[half:]], axis=1)
        sym = lax.dot_general(bins_t2[...], both, dims(1, 1), preferred_element_type=F32)
        expo = jnp.exp(sym - jnp.max(sym, axis=0, keepdims=True))
        probs = expo / jnp.sum(expo, axis=0, keepdims=True)
        labs, scales = [], []
        for u0 in range(0, UNITS, 2):
            (ia, ja), (ib, jb) = places[u0], places[u0 + 1]
            labs.append(
                jnp.where(first_half, lab[ia * col_blocks + ja], lab[ib * col_blocks + jb])
            )
            wa = tab[2, s * UNITS + u0].astype(F32)
            wb = tab[2, s * UNITS + u0 + 1].astype(F32)
            scales.append(jnp.where(first_half, wa, wb))
        labs = jnp.concatenate(labs, axis=1)
        scales = jnp.concatenate(scales, axis=1)
        hit = lax.broadcasted_iota(jnp.int32, sym.shape, 0) == labs
        logit_grad = ((probs - jnp.where(hit, 1.0, 0.0)) * scales).astype(BF16)
        acc_bins[...] += jnp.dot(logit_grad, both, preferred_element_type=F32)
        upd_grad = lax.dot_general(
            logit_grad, bins_t[...], dims(0, 0), preferred_element_type=F32
        )
        upd_half = upd_grad.astype(BF16)
        hid_grad = jnp.dot(upd_half, w_out_t_h[...], preferred_element_type=F32)
        pre_grad = jnp.concatenate(
            [(hid_grad * slope[:half]).astype(BF16), (hid_grad * slope[half:]).astype(BF16)], axis=0
        )
        g_in[...] += lax.dot_general(normed, pre_grad, dims(0, 0), preferred_element_type=F32)
        g_out[...] += lax.dot_general(
            jnp.concatenate([upd_half, upd_half], axis=0), hidden, dims(0, 0),
            preferred_element_type=F32,
        )
        norm_grad = jnp.dot(pre_grad, w_in_t[...], preferred_element_type=F32) * gain_ref[...]
        mean = jnp.sum(norm_grad, axis=-1, keepdims=True) * scale
        mixed = jnp.sum(norm_grad * form, axis=-1, keepdims=True) * scale
        pair = inv * (norm_grad - mean - form * mixed)
        own = (pair[:half] + upd_grad).reshape(UNITS, SUB, SUB, width)
        far = (pair[half:] + upd_grad).reshape(UNITS, SUB, SUB, width)
        for k in range(UNITS):
            acc_li[rows[k]] += own[k]
            o_right_j[cols[k]] += jnp.sum(own[k], axis=0)
            acc_ri[rows[k]] += far[k]
            o_left_j[cols[k]] += jnp.sum(far[k], axis=0)
        return carry

    lax.fori_loop(0, tab[0, last], step, 0)
    o_left_i[...] = jnp.sum(acc_li[...], axis=1)
    o_right_i[...] = jnp.sum(acc_ri[...], axis=1)
    g_bins[...] = acc_bins[:, :width] + acc_bins[:, width:]


def pair_work(tab, left_i, right_i, left_j, right_j, gain, bias, w_in, b_in, w_out, w_bins, labels):
    tile_rows, tile_cols = labels.shape
    width, hidden = w_in.shape
    bins = w_bins.shape[1]
    blocks = labels.reshape(tile_rows // SUB, SUB, tile_cols // SUB, SUB)
    blocks = jnp.transpose(blocks, (0, 2, 1, 3)).reshape(-1, 1, SUB * SUB)
    lab = jnp.concatenate([blocks, blocks], axis=2)
    bins_t = w_bins.T
    half = jnp.asarray(0.5, BF16)
    vmem = pl.BlockSpec(memory_space=pltpu.VMEM)
    shape = jax.ShapeDtypeStruct
    return pl.pallas_call(
        pair_kernel,
        out_shape=(
            shape((width, hidden), F32), shape((width, hidden), F32), shape((bins, width), F32),
            shape((tile_rows, width), F32), shape((tile_rows, width), F32),
            shape((tile_cols, width), F32), shape((tile_cols, width), F32),
        ),
        in_specs=[pl.BlockSpec(memory_space=pltpu.SMEM)] + [vmem] * 14,
        out_specs=(vmem,) * 7,
        scratch_shapes=[pltpu.VMEM((tile_rows, SUB, width), F32)] * 4
        + [pltpu.VMEM((tile_cols, width), F32)] * 4
        + [pltpu.VMEM((tile_rows, SUB, width), F32)] * 2
        + [pltpu.VMEM((bins, 2 * width), F32)],
    )(
        tab, left_i, right_i, left_j, right_j, gain[None], bias[None], w_in * half,
        (b_in * 0.5)[None], w_out, w_in.T, w_out.T * half,
        jnp.concatenate([bins_t, bins_t], axis=1), bins_t, lab,
    )


def on_device(plans, left_act, right_act, norm_gain, norm_bias, w_in, b_in, w_out, w_bins, labels):
    tile_rows, tile_cols = labels.shape
    width = left_act.shape[1]
    row, col = lax.axis_index("row"), lax.axis_index("col")
    stacked = jnp.stack([left_act, right_act])
    everything = lax.all_gather(stacked, ("row", "col"), axis=1, tiled=True)
    residues = everything.shape[1]
    mine = lax.dynamic_slice_in_dim(everything, row * tile_rows, tile_rows, 1)
    theirs = lax.dynamic_slice_in_dim(everything, col * tile_cols, tile_cols, 1)
    tab = lax.dynamic_index_in_dim(plans, row * lax.axis_size("col") + col, 0, keepdims=False)
    g_in, g_out, g_bins, left_i, right_i, left_j, right_j = pair_work(
        tab, mine[0], mine[1], theirs[0], theirs[1], norm_gain, norm_bias, w_in, b_in, w_out,
        w_bins, labels,
    )
    whole = jnp.zeros((2, residues, width), F32)
    by_row = lax.dynamic_update_slice(whole, jnp.stack([left_i, right_i]), (0, row * tile_rows, 0))
    by_col = lax.dynamic_update_slice(whole, jnp.stack([left_j, right_j]), (0, col * tile_cols, 0))
    packed = jnp.concatenate(
        [(by_row + by_col).reshape(-1, width), g_in.reshape(-1, width), g_out.reshape(-1, width),
         g_bins.reshape(-1, width)], axis=0
    )
    total = lax.psum(packed, ("row", "col"))
    own = left_act.shape[0]
    grad_left = lax.dynamic_slice_in_dim(total, (row * lax.axis_size("col") + col) * own, own, 0)
    grad_right = lax.dynamic_slice_in_dim(total, residues + col * tile_cols, tile_cols, 0)
    rest = total[2 * residues :] / residues
    first, second = g_in.size // width, g_out.size // width
    return (
        grad_left,
        grad_right,
        rest[:first].reshape(g_in.shape),
        rest[first : first + second].reshape(g_out.shape).T,
        rest[first + second :].reshape(g_bins.shape).T,
    )


def solution(mesh):
    placed = (
        P(("row", "col"), None),
        P(("row", "col"), None),
        P(),
        P(),
        P(),
        P(),
        P(),
        P(),
        P("row", "col"),
    )
    rows, cols = mesh.shape["row"], mesh.shape["col"]

    def step(*args):
        residues = args[8].shape[0]
        plans = jnp.asarray(schedule(rows, cols, residues // rows, residues // cols))
        return jax.shard_map(
            lambda *local: on_device(plans, *local),
            mesh=mesh,
            in_specs=placed,
            out_specs=(P(("row", "col"), None), P("col", None), P(), P(), P()),
            check_vma=False,
        )(*args)

    return step
```

time: 636 us -> 271 us (0.43)
  matrix products: 222 us -> 0 us
  local copies, waits for them, and re-layouts: 85.1 us -> 12.7 us
  Pallas kernels: 0 us -> 63.5 us
  other arithmetic: 65.9 us -> 8.29 us
  blocking collectives: 81.5 us -> 44.3 us
  waiting for transfers between devices: 158 us -> 127 us
    dot_general x120 -> x0, matrix products: 161 us -> none  [the longest x36 57.6 us: outer(): lax.dot_general(first, second, (((1,), (1,)), ((), ())), preferred_elemen...]
    pallas_call x0 -> x1, Pallas kernels: none -> 63.5 us  [pair_work(): pl.pallas_call(pair_kernel, out_shape=(shape((width, hidden), F32), shape...]
    div x12 -> x0, matrix products: 60.6 us -> none  [pair_backward(): probs = expo / jnp.sum(expo, axis=-1, keepdims=True)]
    psum x1 -> x0, blocking collectives: 37.2 us -> none  [on_device(): lax.psum((running[0], running[1], running[2]), ('row', 'col'))]
    psum x2 -> x1, waiting for transfers between devices: 156 us -> 127 us  [on_device(): total = lax.psum(packed, ('row', 'col'))]
    reshape x24 -> x8, local copies, waits for them, and re-layouts: 28.3 us -> 4.33 us  [the longest x1 1.04 us: on_device(): g_in.reshape(-1, width)]
    add x36 -> x1, other arithmetic: 23.4 us -> 0.04 us  [on_device(): by_row + by_col]
    reduce_sum x60 -> x0, other arithmetic: 21.4 us -> none  [the longest x24 13.1 us: transition(): jnp.mean(center * center, axis=-1, keepdims=True) + 1e-05]
  transfers between devices with their start and end apart: 3 -> 1, of which waited for: 2 -> 1; matrix products, arithmetic and copies ran while one was open for 1% -> 0% of each run, Pallas kernels for 0% -> 0%
where the time goes in v1:
time: 271 us; the launch traced here: 270 us
  waiting for transfers between devices  127 us (47%)
  Pallas kernels  63.5 us (23%)
  blocking collectives  44.3 us (16%)
  between operations  14.2 us (5%)
  local copies, waits for them, and re-layouts  12.7 us (5%)
  other arithmetic  8.29 us (3%)
    psum x1, waiting for transfers between devices, on_device(): total = lax.psum(packed, ('row', 'col'))  127 us
    pallas_call x1, Pallas kernels, pair_work(): pl.pallas_call(pair_kernel, out_shape=(shape((width, hidden), F32), shape...  63.5 us
    all_gather x1, blocking collectives, on_device(): everything = lax.all_gather(stacked, ('row', 'col'), axis=1, tiled=True)  44.3 us
  transfers between devices with their start and end apart: 1, of which 1 were waited for; matrix products, arithmetic and copies ran while one was open for 0% of the time, Pallas kernels for 0%

profile of v1, /device:TPU:0, one launch (start us, length us, event | category | flops | bytes accessed | tf_op | source)
XLA Modules:
  0.0 270.3 jit_solution(458592301393648329)
XLA Ops:
  7.2 0.0 copy-start.1
  7.2 0.0 all-reduce.2.cloned.1.call-start
  7.2 1.7 copy.19
  8.9 1.6 broadcast_multiply_fusion.w_in_h
  10.5 0.7 pad_maximum_fusion.2
  11.2 44.3 %all_gather.3 = bf16[2,768,128]{2,1,0:T(8,128)(2,1)S(1)} all-gather(bf16[2,24,128]{2,1,0:T(8,128)(2,1)S(1)} %pad_maximum_fusion.2), channel_id=1, replica_groups=mesh['row'=8,'col'=4] {'row','col'}, dimensions={1}, use_global_device_ids=true | all-gather | bytes 405504 | tf_op jit(solution)/shard_map/all_gather | solution.py:178
  55.5 0.6 dynamic-slice_bitcast_fusion
  56.1 0.6 dynamic-slice_bitcast_fusion.2
  56.7 1.4 pad_maximum_fusion.1.bins_t2
  58.1 0.0 copy-done.1
  58.1 0.4 reshape.31
  58.5 0.0 copy-start
  58.6 0.0 copy-start.7
  58.6 0.5 copy.21
  59.1 0.2 reshape.32
  59.3 0.1 copy.22
  59.4 1.0 pad_add_fusion.lab
  60.4 0.0 copy-done
  60.4 0.1 copy.20
  60.5 0.7 multiply_bitcast_fusion.w_out_t_h
  61.2 0.0 copy-done.7
  61.2 0.6 broadcast_multiply_fusion.1
  61.8 1.3 dynamic-slice_bitcast_fusion.4.tab
  63.1 63.5 %shard_map.137 = (f32[128,512]{1,0:T(8,128)}, f32[128,512]{1,0:T(8,128)}, f32[64,128]{1,0:T(8,128)}, f32[96,128]{1,0:T(8,128)}, f32[96,128]{1,0:T(8,128)}, /*index=5*/f32[192,128]{1,0:T(8,128)}, f32[192,128]{1,0:T(8,128)}) custom-call(s32[3,151]{1,0:T(4,128)} %dynamic-slice_bitcast_fusion.4.tab, bf16[96,128]{1,0:T(8,128)(2,1)} %get-tuple-element.24.left_i, ...), custom_call_target="tpu_custom_call" | custom-call | tf_op jit(solution)/shard_map/pallas_call | solution.py:153
  126.6 0.0 copy-start.4
  126.6 0.0 copy-start.5
  126.6 0.0 copy-start.2
  126.6 0.0 copy-start.3
  126.6 0.0 copy-start.6
  126.6 1.0 reshape.34
  127.7 1.0 reshape.35
  128.6 0.1 broadcast_in_dim.12
  128.7 0.0 copy-done.4
  128.7 0.0 copy-done.5
  128.7 0.0 copy-done.2
  128.7 0.0 copy-done.3
  128.8 0.0 copy-done.6
  128.8 1.2 pad_maximum_fusion
  130.0 0.0 all-reduce.2.cloned.1.call-update
  130.0 127.2 %all-reduce.2.cloned.1.call-done = f32[2624,128]{1,0:T(8,128)} async-done(((f32[2624,128]{1,0:T(8,128)}), f32[2624,128]{1,0:T(8,128)}) %all-reduce.2.cloned.1.call-update) | async-done | bytes 1343504 | tf_op jit(solution)/shard_map/psum | solution.py:194
  257.2 1.1 slice_multiply_fusion
  258.4 0.6 slice_bitcast_fusion
  259.1 0.8 copy.24
  259.9 0.7 reshape.36
  260.6 1.5 constant_dynamic-slice_fusion
  262.2 1.3 constant_dynamic-slice_fusion.1
  (4 shorter events, 0.1 us)
Async XLA Ops:
  7.2 51.0 %copy-start.1 = (s32[96,192]{1,0:T(8,128)S(1)}, s32[96,192]{1,0:T(8,128)}, u32[]{:S(2)}) copy-start(s32[96,192]{1,0:T(8,128)} %param.18) | copy-start | bytes 221188
  7.2 250.1 %all-reduce.2.cloned.1.call-start = ((), (), s32[]{:S(2)}) async-start(), calls=%async_computation | async-start | bytes 2686976 | tf_op jit(solution)/shard_map/psum | solution.py:194
  58.5 1.9 copy-start
  58.6 2.7 copy-start.7
  126.6 2.1 copy-start.4
  126.6 2.1 copy-start.5
  126.6 2.2 copy-start.2
  126.6 2.1 copy-start.3
  126.6 2.2 copy-start.6
Sparse Core Ops, SparseCore 0:
  130.1 127.0 all-reduce.1

commit v2 on v1

--- a/solution.py
+++ b/solution.py
@@ -1,3 +1,5 @@
+import functools
+
 import jax
 import jax.numpy as jnp
 import numpy as np
@@ -39,26 +41,40 @@
 
 
 def pair_kernel(
-    tab, left_i, right_i, left_j, right_j, gain_ref, bias_ref, w_in_h, b_h, w_out_ref, w_in_t,
-    w_out_t_h, bins_t2, bins_t, lab,
-    g_in, g_out, g_bins, o_left_i, o_right_i, o_left_j, o_right_j,
-    raw_li, raw_ri, cen_li, cen_ri, raw_lj, raw_rj, cen_lj, cen_rj, acc_li, acc_ri, acc_bins,
+    tab, row_in, col_in, gain_ref, bias_ref, w_in_ref, b_ref, w_out_ref, w_bins_ref, lab,
+    packed, res_i, res_j,
+    w_in_h, b_h, w_in_t, w_out_t_h, bins_t2, bins_t, raw_li, raw_ri, cen_li, cen_ri, raw_lj,
+    raw_rj, cen_lj, cen_rj, acc_li, acc_ri, o_left_j, o_right_j, g_in, g_out, acc_bins,
 ):
     width = gain_ref.shape[1]
     scale = 1.0 / width
     half = UNITS * SUB * SUB
     last = tab.shape[1] - 1
-    col_blocks = left_j.shape[0] // SUB
-
-    for source, raw, cen in ((left_i, raw_li, cen_li), (right_i, raw_ri, cen_ri)):
-        value = source[...].astype(F32)
+    col_blocks = raw_lj.shape[0] // SUB
+
+    chunk = row_in.shape[2]
+
+    def whole(source, side):
+        parts = [source[k, side].astype(F32) for k in range(source.shape[0])]
+        return jnp.concatenate(parts, axis=0)
+
+    for side, raw, cen in ((0, raw_li, cen_li), (1, raw_ri, cen_ri)):
+        value = whole(row_in, side)
         mid = value - jnp.sum(value, axis=-1, keepdims=True) * scale
         raw[...] = jnp.broadcast_to(value[:, None, :], raw.shape)
         cen[...] = jnp.broadcast_to(mid[:, None, :], cen.shape)
-    for source, raw, cen in ((left_j, raw_lj, cen_lj), (right_j, raw_rj, cen_rj)):
-        value = source[...].astype(F32)
+    for side, raw, cen in ((0, raw_lj, cen_lj), (1, raw_rj, cen_rj)):
+        value = whole(col_in, side)
         raw[...] = value
         cen[...] = value - jnp.sum(value, axis=-1, keepdims=True) * scale
+    w_in = w_in_ref[...].astype(F32)
+    w_in_h[...] = (w_in * 0.5).astype(BF16)
+    w_in_t[...] = w_in.T.astype(BF16)
+    b_h[...] = b_ref[...] * 0.5
+    w_out_t_h[...] = (w_out_ref[...].astype(F32) * 0.5).T.astype(BF16)
+    turned = w_bins_ref[...].astype(F32).T.astype(BF16)
+    bins_t[...] = turned
+    bins_t2[...] = jnp.concatenate([turned, turned], axis=1)
     for ref in (g_in, g_out, acc_bins, o_left_j, o_right_j, acc_li, acc_ri):
         ref[...] = jnp.zeros_like(ref)
 
@@ -134,76 +150,291 @@
         return carry
 
     lax.fori_loop(0, tab[0, last], step, 0)
-    o_left_i[...] = jnp.sum(acc_li[...], axis=1)
-    o_right_i[...] = jnp.sum(acc_ri[...], axis=1)
-    g_bins[...] = acc_bins[:, :width] + acc_bins[:, width:]
-
-
-def pair_work(tab, left_i, right_i, left_j, right_j, gain, bias, w_in, b_in, w_out, w_bins, labels):
+    for side, acc in ((0, acc_li), (1, acc_ri)):
+        value = jnp.sum(acc[...], axis=1)
+        for k in range(res_i.shape[0]):
+            res_i[k, side] = value[k * chunk : (k + 1) * chunk]
+    for side, acc in ((0, o_left_j), (1, o_right_j)):
+        for k in range(res_j.shape[0]):
+            res_j[k, side] = acc[k * chunk : (k + 1) * chunk]
+    hidden_width = g_in.shape[1]
+    for k in range(hidden_width // width):
+        packed[k * width : (k + 1) * width] = g_in[:, k * width : (k + 1) * width]
+    packed[hidden_width : 2 * hidden_width] = g_out[...].T
+    end = 2 * hidden_width + acc_bins.shape[0]
+    packed[2 * hidden_width : end] = acc_bins[:, :width] + acc_bins[:, width:]
+    if end < packed.shape[0]:
+        packed[end:] = jnp.zeros((packed.shape[0] - end, width), F32)
+
+
+def pair_work(tab, row_in, col_in, gain, bias, w_in, b_in, w_out, w_bins, labels, packed_rows):
     tile_rows, tile_cols = labels.shape
     width, hidden = w_in.shape
     bins = w_bins.shape[1]
     blocks = labels.reshape(tile_rows // SUB, SUB, tile_cols // SUB, SUB)
     blocks = jnp.transpose(blocks, (0, 2, 1, 3)).reshape(-1, 1, SUB * SUB)
     lab = jnp.concatenate([blocks, blocks], axis=2)
-    bins_t = w_bins.T
-    half = jnp.asarray(0.5, BF16)
     vmem = pl.BlockSpec(memory_space=pltpu.VMEM)
     shape = jax.ShapeDtypeStruct
     return pl.pallas_call(
         pair_kernel,
         out_shape=(
-            shape((width, hidden), F32), shape((width, hidden), F32), shape((bins, width), F32),
-            shape((tile_rows, width), F32), shape((tile_rows, width), F32),
-            shape((tile_cols, width), F32), shape((tile_cols, width), F32),
+            shape((packed_rows, width), F32), shape(row_in.shape, F32), shape(col_in.shape, F32),
         ),
-        in_specs=[pl.BlockSpec(memory_space=pltpu.SMEM)] + [vmem] * 14,
-        out_specs=(vmem,) * 7,
-        scratch_shapes=[pltpu.VMEM((tile_rows, SUB, width), F32)] * 4
+        in_specs=[pl.BlockSpec(memory_space=pltpu.SMEM)] + [vmem] * 9,
+        out_specs=(vmem,) * 3,
+        scratch_shapes=[
+            pltpu.VMEM((width, hidden), BF16), pltpu.VMEM((1, hidden), F32),
+            pltpu.VMEM((hidden, width), BF16), pltpu.VMEM((width, hidden), BF16),
+            pltpu.VMEM((bins, 2 * width), BF16), pltpu.VMEM((bins, width), BF16),
+        ]
+        + [pltpu.VMEM((tile_rows, SUB, width), F32)] * 4
         + [pltpu.VMEM((tile_cols, width), F32)] * 4
         + [pltpu.VMEM((tile_rows, SUB, width), F32)] * 2
+        + [pltpu.VMEM((tile_cols, width), F32)] * 2
+        + [pltpu.VMEM((width, hidden), F32)] * 2
         + [pltpu.VMEM((bins, 2 * width), F32)],
-    )(
-        tab, left_i, right_i, left_j, right_j, gain[None], bias[None], w_in * half,
-        (b_in * 0.5)[None], w_out, w_in.T, w_out.T * half,
-        jnp.concatenate([bins_t, bins_t], axis=1), bins_t, lab,
+        name="pairs",
+    )(tab, row_in, col_in, gain[None], bias[None], w_in, b_in[None], w_out, w_bins, lab)
+
+
+def partners(rows, cols):
+    r, c = lax.axis_index("row"), lax.axis_index("col")
+    place = r * cols + c
+    home = place // rows
+    slot = place % rows
+
+    def owner(m):
+        k = c * rows + m
+        return (k // cols, k % cols)
+
+    return r, c, home, slot, owner
+
+
+def unless(skip, action):
+    if skip is None:
+        action()
+    else:
+        pl.when(jnp.logical_not(skip))(action)
+
+
+def greet(rows, cols, with_column):
+    r, c, home, slot, owner = partners(rows, cols)
+    barrier = pltpu.get_barrier_semaphore()
+
+    def hello(device, skip):
+        unless(skip, lambda: pl.semaphore_signal(
+            barrier, inc=1, device_id=device, device_id_type=pl.DeviceIdType.MESH))
+
+    for k in range(cols):
+        hello((r, k), k == c)
+    for k in range(rows):
+        if with_column:
+            hello((k, c), k == r)
+        hello((k, home), jnp.logical_and(k == r, home == c))
+        hello(owner(k), jnp.logical_and(home == c, k == slot))
+    count = cols - 1 + 2 * rows + (rows - 1 if with_column else 0)
+    pl.semaphore_wait(barrier, count - 2 * jnp.where(home == c, 1, 0))
+
+
+def remote(src, dst, send, recv, device):
+    return pltpu.make_async_remote_copy(
+        src_ref=src, dst_ref=dst, send_sem=send, recv_sem=recv, device_id=device,
+        device_id_type=pl.DeviceIdType.MESH,
     )
 
 
+def gather_kernel(rows, cols, left, right, row_out, col_out, s_row, r_row, s_col, r_col):
+    r, c, home, slot, owner = partners(rows, cols)
+    here = home == c
+    greet(rows, cols, False)
+    sides = ((0, left), (1, right))
+
+    def row_copy(side, src, k, at):
+        return remote(src, row_out.at[at, side], s_row.at[k, side], r_row.at[at, side], (r, k))
+
+    def col_copy(side, src, k, at, device):
+        return remote(src, col_out.at[at, side], s_col.at[k, side], r_col.at[at, side], device)
+
+    for side, src in sides:
+        for k in range(rows):
+            unless(jnp.logical_and(here, k == r),
+                   lambda: col_copy(side, src, k, slot, (k, home)).start())
+        for k in range(cols):
+            unless(k == c, lambda: row_copy(side, src, k, c).start())
+    for side, src in sides:
+        row_out[c, side] = src[...]
+
+        @pl.when(here)
+        def _():
+            col_out[slot, side] = src[...]
+
+    for side, src in sides:
+        for k in range(cols):
+            unless(k == c, lambda: row_copy(side, src, k, k).wait_recv())
+        for k in range(rows):
+            unless(jnp.logical_and(here, k == slot),
+                   lambda: col_copy(side, src, k, k, owner(k)).wait_recv())
+    for side, src in sides:
+        for k in range(cols):
+            unless(k == c, lambda: row_copy(side, src, k, c).wait_send())
+        for k in range(rows):
+            unless(jnp.logical_and(here, k == r),
+                   lambda: col_copy(side, src, k, slot, (k, home)).wait_send())
+
+
+def reduce_kernel(
+    rows, cols, residues, mine, res_i, res_j, o_left, o_right, o_in, o_out, o_bins,
+    got1, sum1, got2, total, got_i, got_j, right_sum,
+    s1, r1, s2, r2, s3, r3, s4, r4, si, ri, sj, rj, sb, rb,
+):
+    r, c, home, slot, owner = partners(rows, cols)
+    here = home == c
+    greet(rows, cols, True)
+    width = total.shape[-1]
+
+    def one(k, at):
+        return remote(mine.at[k], got1.at[at], s1.at[k], r1.at[at], (r, k))
+
+    def two(k, at):
+        return remote(sum1.at[k], got2.at[at], s2.at[k], r2.at[at], (k, c))
+
+    def three(k, at):
+        return remote(total.at[c, r], total.at[c, at], s3.at[k], r3.at[at], (k, c))
+
+    def four(k, at):
+        return remote(total.at[c], total.at[at], s4.at[k], r4.at[at], (r, k))
+
+    def share_i(k, at):
+        return remote(res_i.at[k], got_i.at[at], si.at[k], ri.at[at], (r, k))
+
+    def share_j(k, at, device):
+        return remote(res_j.at[k], got_j.at[at], sj.at[k], rj.at[at], device)
+
+    def spread(k, at, device):
+        return remote(right_sum, o_right.at[at], sb.at[k], rb.at[at], device)
+
+    for k in range(cols):
+        unless(k == c, lambda: one(k, c).start())
+    for k in range(cols):
+        unless(k == c, lambda: share_i(k, c).start())
+    for k in range(rows):
+        unless(jnp.logical_and(here, k == slot), lambda: share_j(k, r, owner(k)).start())
+    got1[c] = mine[c]
+    got_i[c] = res_i[c]
+
+    @pl.when(here)
+    def _():
+        got_j[r] = res_j[slot]
+
+    for k in range(cols):
+        unless(k == c, lambda: one(k, k).wait_recv())
+    acc = got1[0]
+    for k in range(1, cols):
+        acc = acc + got1[k]
+    sum1[...] = acc
+    for k in range(rows):
+        unless(k == r, lambda: two(k, r).start())
+    got2[r] = sum1[r]
+    for k in range(cols):
+        unless(k == c, lambda: share_i(k, k).wait_recv())
+    for k in range(rows):
+        unless(jnp.logical_and(here, k == r), lambda: share_j(k, k, (k, home)).wait_recv())
+    both = got_i[0]
+    for k in range(1, cols):
+        both = both + got_i[k]
+    for k in range(rows):
+        both = both + got_j[k]
+    o_left[...] = both[0]
+
+    for k in range(rows):
+        unless(k == r, lambda: two(k, k).wait_recv())
+    acc = got2[0]
+    for k in range(1, rows):
+        acc = acc + got2[k]
+    total[c, r] = acc
+    for k in range(rows):
+        unless(k == r, lambda: three(k, r).start())
+    right_sum[...] = both[1]
+
+    @pl.when(here)
+    def _():
+        o_right[slot] = both[1]
+
+    for k in range(rows):
+        unless(jnp.logical_and(here, k == r), lambda: spread(k, slot, (k, home)).start())
+    for k in range(rows):
+        unless(k == r, lambda: three(k, k).wait_recv())
+    for k in range(cols):
+        unless(k == c, lambda: four(k, c).start())
+    for k in range(cols):
+        unless(k == c, lambda: four(k, k).wait_recv())
+    flat = total[...].reshape(-1, width) * (1.0 / residues)
+    hidden_width = o_in.shape[1]
+    for k in range(hidden_width // width):
+        o_in[:, k * width : (k + 1) * width] = flat[k * width : (k + 1) * width]
+    o_out[...] = flat[hidden_width : 2 * hidden_width]
+    o_bins[...] = flat[2 * hidden_width : 2 * hidden_width + o_bins.shape[1]].T
+    for k in range(rows):
+        unless(jnp.logical_and(here, k == slot), lambda: spread(k, k, owner(k)).wait_recv())
+    for k in range(cols):
+        unless(k == c, lambda: one(k, c).wait_send())
+        unless(k == c, lambda: share_i(k, c).wait_send())
+        unless(k == c, lambda: four(k, c).wait_send())
+    for k in range(rows):
+        unless(k == r, lambda: two(k, r).wait_send())
+        unless(k == r, lambda: three(k, r).wait_send())
+        unless(jnp.logical_and(here, k == slot), lambda: share_j(k, r, owner(k)).wait_send())
+        unless(jnp.logical_and(here, k == r), lambda: spread(k, slot, (k, home)).wait_send())
+
+
 def on_device(plans, left_act, right_act, norm_gain, norm_bias, w_in, b_in, w_out, w_bins, labels):
-    tile_rows, tile_cols = labels.shape
-    width = left_act.shape[1]
-    row, col = lax.axis_index("row"), lax.axis_index("col")
-    stacked = jnp.stack([left_act, right_act])
-    everything = lax.all_gather(stacked, ("row", "col"), axis=1, tiled=True)
-    residues = everything.shape[1]
-    mine = lax.dynamic_slice_in_dim(everything, row * tile_rows, tile_rows, 1)
-    theirs = lax.dynamic_slice_in_dim(everything, col * tile_cols, tile_cols, 1)
-    tab = lax.dynamic_index_in_dim(plans, row * lax.axis_size("col") + col, 0, keepdims=False)
-    g_in, g_out, g_bins, left_i, right_i, left_j, right_j = pair_work(
-        tab, mine[0], mine[1], theirs[0], theirs[1], norm_gain, norm_bias, w_in, b_in, w_out,
-        w_bins, labels,
+    rows, cols = lax.axis_size("row"), lax.axis_size("col")
+    chunk, width = left_act.shape
+    hidden, bins = w_in.shape[1], w_bins.shape[1]
+    residues = chunk * rows * cols
+    vmem = pl.BlockSpec(memory_space=pltpu.VMEM)
+    shape = jax.ShapeDtypeStruct
+    dma = pltpu.SemaphoreType.DMA
+    row_in, col_in = pl.pallas_call(
+        functools.partial(gather_kernel, rows, cols),
+        out_shape=(shape((cols, 2, chunk, width), BF16), shape((rows, 2, chunk, width), BF16)),
+        in_specs=[vmem] * 2,
+        out_specs=(vmem,) * 2,
+        scratch_shapes=[dma((cols, 2)), dma((cols, 2)), dma((rows, 2)), dma((rows, 2))],
+        compiler_params=pltpu.CompilerParams(collective_id=0, has_side_effects=True),
+        name="gather",
+    )(left_act, right_act)
+    tab = lax.dynamic_index_in_dim(
+        plans, lax.axis_index("row") * cols + lax.axis_index("col"), 0, keepdims=False
     )
-    whole = jnp.zeros((2, residues, width), F32)
-    by_row = lax.dynamic_update_slice(whole, jnp.stack([left_i, right_i]), (0, row * tile_rows, 0))
-    by_col = lax.dynamic_update_slice(whole, jnp.stack([left_j, right_j]), (0, col * tile_cols, 0))
-    packed = jnp.concatenate(
-        [(by_row + by_col).reshape(-1, width), g_in.reshape(-1, width), g_out.reshape(-1, width),
-         g_bins.reshape(-1, width)], axis=0
+    piece = -(-(2 * hidden + bins) // (rows * cols * SUB)) * SUB
+    packed, res_i, res_j = pair_work(
+        tab, row_in, col_in, norm_gain, norm_bias, w_in, b_in, w_out, w_bins, labels,
+        rows * cols * piece,
     )
-    total = lax.psum(packed, ("row", "col"))
-    own = left_act.shape[0]
-    grad_left = lax.dynamic_slice_in_dim(total, (row * lax.axis_size("col") + col) * own, own, 0)
-    grad_right = lax.dynamic_slice_in_dim(total, residues + col * tile_cols, tile_cols, 0)
-    rest = total[2 * residues :] / residues
-    first, second = g_in.size // width, g_out.size // width
-    return (
-        grad_left,
-        grad_right,
-        rest[:first].reshape(g_in.shape),
-        rest[first : first + second].reshape(g_out.shape).T,
-        rest[first + second :].reshape(g_bins.shape).T,
-    )
+    packed = packed.reshape(cols, rows, piece, width)
+    part = packed.shape[1:]
+    grad_left, grad_right, grad_in, grad_out, grad_bins = pl.pallas_call(
+        functools.partial(reduce_kernel, rows, cols, residues),
+        out_shape=(
+            shape((chunk, width), F32), shape((rows, chunk, width), F32),
+            shape((width, hidden), F32), shape((hidden, width), F32), shape((width, bins), F32),
+        ),
+        in_specs=[vmem] * 3,
+        out_specs=(vmem,) * 5,
+        scratch_shapes=[
+            pltpu.VMEM(packed.shape, F32), pltpu.VMEM(part, F32), pltpu.VMEM(part, F32),
+            pltpu.VMEM(packed.shape, F32), pltpu.VMEM(res_i.shape, F32),
+            pltpu.VMEM(res_j.shape, F32), pltpu.VMEM((chunk, width), F32),
+            dma((cols,)), dma((cols,)), dma((rows,)), dma((rows,)), dma((rows,)), dma((rows,)),
+            dma((cols,)), dma((cols,)), dma((cols,)), dma((cols,)), dma((rows,)), dma((rows,)),
+            dma((rows,)), dma((rows,)),
+        ],
+        compiler_params=pltpu.CompilerParams(collective_id=1, has_side_effects=True),
+        name="reduce",
+    )(packed, res_i, res_j)
+    return (grad_left, grad_right.reshape(-1, width), grad_in, grad_out, grad_bins)
 
 
 def solution(mesh):

time: 271 us -> 122 us (0.45)
  waiting for transfers between devices: 127 us -> 0 us
  blocking collectives: 44.3 us -> 0 us
  Pallas kernels: 63.5 us -> 107 us
  between operations: 14.2 us -> 0.68 us
  other arithmetic: 8.29 us -> 1.04 us
    psum x1 -> x0, waiting for transfers between devices: 127 us -> none  [on_device(): total = lax.psum(packed, ('row', 'col'))]
    all_gather x1 -> x0, blocking collectives: 44.3 us -> none  [on_device(): everything = lax.all_gather(stacked, ('row', 'col'), axis=1, tiled=True)]
    pallas_call x1 -> x3, Pallas kernels: 63.5 us -> 107 us  [the longest x1 63.6 us: pair_work(): pl.pallas_call(pair_kernel, out_shape=(shape((packed_rows, width), F32),...]
    unnamed x18 -> x8, local copies, waits for them, and re-layouts: 1.81 us -> 8.45 us
    reshape x5 -> x0, local copies, waits for them, and re-layouts: 3.63 us -> none  [the longest x1 1.04 us: on_device(): g_in.reshape(-1, width)]
    dynamic_slice x2 -> x0, local copies, waits for them, and re-layouts: 2.84 us -> none  [the longest x1 1.54 us: on_device(): lax.dynamic_slice_in_dim(total, residues + col * tile_cols, tile_cols, 0)]
    mul x3 -> x0, other arithmetic: 2.79 us -> none  [the longest x1 1.56 us: pair_work(): w_in * half]
  transfers between devices with their start and end apart: 1 -> 0, of which waited for: 1 -> 0; matrix products, arithmetic and copies ran while one was open for 0% -> 0% of each run, Pallas kernels for 0% -> 0%
where the time goes in v2:
time: 122 us; the launch traced here: 121 us
  Pallas kernels  107 us (88%)
  local copies, waits for them, and re-layouts  11.8 us (10%)
    pallas_call x1, Pallas kernels, pair_work(): pl.pallas_call(pair_kernel, out_shape=(shape((packed_rows, width), F32),...  63.6 us
    pallas_call x1, Pallas kernels, on_device(): pl.pallas_call(functools.partial(reduce_kernel, rows, cols, residues), ou...  32 us
    pallas_call x1, Pallas kernels, on_device(): pl.pallas_call(functools.partial(gather_kernel, rows, cols), out_shape=(s...  11.8 us
    unnamed x8, local copies, waits for them, and re-layouts  8.45 us

profile of v2, /device:TPU:0, one launch (start us, length us, event | category | flops | bytes accessed | tf_op | source)
XLA Modules:
  0.0 121.0 jit_solution(16019228181526295422)
XLA Ops:
  0.6 1.3 %dynamic-slice_bitcast_fusion.tab = s32[3,151]{1,0:T(4,128)} fusion(s32[32,3,151]{2,1,0:T(4,128)} %constant.19.clone, s32[]{:T(128)S(6)} %select_n.4), kind=kLoop, calls=%fused_computation.1 | loop fusion | bytes 3628 | tf_op jit(solution)/shard_map/jit(dynamic_index_in_dim)/squeeze | solution.py:408
  1.9 11.8 %gather.1 = (bf16[4,2,24,128]{3,2,1,0:T(8,128)(2,1)}, bf16[8,2,24,128]{3,2,1,0:T(8,128)(2,1)}) custom-call(bf16[24,128]{1,0:T(8,128)(2,1)} %left.1, bf16[24,128]{1,0:T(8,128)(2,1)} %right.1), custom_call_target="tpu_custom_call" | custom-call | tf_op jit(solution)/shard_map/gather/pallas_call | solution.py:399
  13.8 1.3 %reshape.22 = s32[12,8,24,8]{3,2,1,0:T(8,128)S(1)} reshape(s32[96,192]{1,0:T(8,128)} %param.18) | data formatting | bytes 147456 | tf_op jit(solution)/shard_map/reshape | solution.py:174
  15.1 0.0 copy-start
  15.1 0.5 copy.18
  15.6 0.2 reshape.23
  15.8 0.1 copy.19
  15.9 1.0 pad_add_fusion.lab
  16.9 0.0 copy-done
  16.9 0.7 copy.21.w_bins_ref
  17.7 63.6 %pairs.1 = (f32[1280,128]{1,0:T(8,128)}, f32[4,2,24,128]{3,2,1,0:T(8,128)}, f32[8,2,24,128]{3,2,1,0:T(8,128)}) custom-call(s32[3,151]{1,0:T(4,128)} %dynamic-slice_bitcast_fusion.tab, bf16[4,2,24,128]{3,2,1,0:T(8,128)(2,1)} %get-tuple-element.15.row_in, bf16[8,2,24,128]{3,2,1,0:T(8,128)(2,1)} %get-tuple-element.16.col_in, f32[1,128]{1,0:T(1,128)} %bitcast.14, ...), custom_call_target="tpu_custom_call" | custom-call | tf_op jit(solution)/shard_map/pairs/pallas_call | solution.py:179
  81.2 32.0 %reduce.1 = (f32[24,128]{1,0:T(8,128)}, f32[8,24,128]{2,1,0:T(8,128)}, f32[128,512]{1,0:T(8,128)}, f32[512,128]{1,0:T(8,128)}, f32[128,64]{1,0:T(8,128)}) custom-call(f32[4,8,40,128]{3,2,1,0:T(8,128)} %bitcast.11, f32[4,2,24,128]{3,2,1,0:T(8,128)} %get-tuple-element.18.res_i, f32[8,2,24,128]{3,2,1,0:T(8,128)} %get-tuple-element.19.res_j), custom_call_target="tpu_custom_call" | custom-call | tf_op jit(solution)/shard_map/reduce/pallas_call | solution.py:418
  113.3 1.5 %copy.22 = f32[128,64]{0,1:T(8,128)} copy(f32[128,64]{1,0:T(8,128)} %get-tuple-element.34) | data formatting | bytes 65536
  114.8 1.3 %copy.27 = f32[24,128]{1,0:T(8,128)} copy(f32[24,128]{1,0:T(8,128)} %get-tuple-element.40) | data formatting | bytes 24576
  116.1 1.5 %copy.28 = f32[192,128]{1,0:T(8,128)} copy(f32[192,128]{1,0:T(8,128)} %bitcast.12) | data formatting | bytes 196608
  117.6 1.7 %copy.29 = f32[128,512]{1,0:T(8,128)} copy(f32[128,512]{1,0:T(8,128)} %get-tuple-element.42) | data formatting | bytes 524288
  119.3 1.7 %copy.30 = f32[512,128]{1,0:T(8,128)} copy(f32[512,128]{1,0:T(8,128)} %get-tuple-element.43) | data formatting | bytes 524288
Async XLA Ops:
  15.1 1.9 %copy-start = (bf16[128,64]{0,1:T(8,128)(2,1)S(1)}, bf16[128,64]{0,1:T(8,128)(2,1)}, u32[]{:S(2)}) copy-start(bf16[128,64]{0,1:T(8,128)(2,1)} %param.17) | copy-start | bytes 49156
